TPU v7x, 32 devices: a whole 2x2x4 slice. The times are simulated.
32 devices in a mesh: fsdp: 8 (over y, x, core), seq: 4 (over z).
Axes of the slice: x: 2, y: 2, z: 4, core: 2. Of those that a mesh axis runs over, the one named last changes fastest.
Arguments:
- inputs: bfloat16 [8, 1568, 1024], P('fsdp', 'seq'), may hold values from -6 to 6
- clip_mask: int32 [8], P('fsdp'), may hold values 0 or 1
- ln1_gain: float32 [1024], replicated, may hold values from 0.5 to 1.5
- ln1_bias: float32 [1024], replicated, may hold values from -1 to 1
- w_query: bfloat16 [1024, 1024], P('fsdp'), may hold values from -0.1875 to 0.1875
- b_query: float32 [1024], replicated, may hold values from -1 to 1
- w_key: bfloat16 [1024, 1024], P('fsdp'), may hold values from -0.1875 to 0.1875
- w_value: bfloat16 [1024, 1024], P('fsdp'), may hold values from -0.1875 to 0.1875
- b_value: float32 [1024], replicated, may hold values from -1 to 1
- w_out: bfloat16 [1024, 1024], P('fsdp'), may hold values from -3 to 3
- b_out: float32 [1024], replicated, may hold values from -1 to 1
- ln2_gain: float32 [1024], replicated, may hold values from 0.5 to 1.5
- ln2_bias: float32 [1024], replicated, may hold values from -1 to 1
- w_fc1: bfloat16 [1024, 4096], P('fsdp'), may hold values from -0.1875 to 0.1875
- b_fc1: float32 [4096], replicated, may hold values from -1 to 1
- w_fc2: bfloat16 [4096, 1024], P('fsdp'), may hold values from -0.09375 to 0.09375
- b_fc2: float32 [1024], replicated, may hold values from -1 to 1
- cotangent: bfloat16 [8, 1568, 1024], P('fsdp', 'seq'), may hold values from -6 to 6
Outputs:
- output: bfloat16 [8, 1568, 1024], P('fsdp', 'seq')
- grad_inputs: float32 [8, 1568, 1024], P('fsdp', 'seq')
- grad_ln1_gain: float32 [1024], P(('fsdp', 'seq'))
- grad_ln1_bias: float32 [1024], P(('fsdp', 'seq'))
- grad_w_query: float32 [1024, 1024], P(('fsdp', 'seq'))
- grad_b_query: float32 [1024], P(('fsdp', 'seq'))
- grad_w_key: float32 [1024, 1024], P(('fsdp', 'seq'))
- grad_w_value: float32 [1024, 1024], P(('fsdp', 'seq'))
- grad_b_value: float32 [1024], P(('fsdp', 'seq'))
- grad_w_out: float32 [1024, 1024], P(('fsdp', 'seq'))
- grad_b_out: float32 [1024], P(('fsdp', 'seq'))
- grad_ln2_gain: float32 [1024], P(('fsdp', 'seq'))
- grad_ln2_bias: float32 [1024], P(('fsdp', 'seq'))
- grad_w_fc1: float32 [1024, 4096], P(('fsdp', 'seq'))
- grad_b_fc1: float32 [4096], P(('fsdp', 'seq'))
- grad_w_fc2: float32 [4096, 1024], P(('fsdp', 'seq'))
- grad_b_fc2: float32 [1024], P(('fsdp', 'seq'))
Inputs may be any that keep to these rules, and one draw needn't show every extreme that they name: `clip_mask`: 1 where the clip's slot holds a clip, 0 where it holds none.
All inputs are finite; a program needn't handle non-finite values. No bound on the sum of `clip_mask` on one device may be relied on, other than what follows from the above.
Results may differ from a plain program's by a relative error of at most 0.011.
Values may be sent and summed in bfloat16 or wider, within the bound.
No kernel may reach another device: no remote copies, remote signals or barrier semaphores. Data moves between devices by JAX's collectives and lax.ppermute only.
A program may use at most 256 MiB of HBM per device.

v0:
```python
import jax
import jax.numpy as jnp
from jax import lax
from jax.sharding import PartitionSpec as P

HEADS = 16
HD = 64
EPSILON = 1e-06


def normalize(rows, gain, shift):
    center = rows - jnp.mean(rows, -1, keepdims=True)
    inverse = lax.rsqrt(jnp.mean(center * center, -1, keepdims=True) + EPSILON)
    normed = center * inverse
    return (normed * gain + shift, normed, inverse)


def norm_grad(grad, normed, inverse, gain):
    scaled = grad * gain
    inner = (
        scaled
        - jnp.mean(scaled, -1, keepdims=True)
        - normed * jnp.mean(scaled * normed, -1, keepdims=True)
    )
    return inner * inverse


def to_pairs(array):
    clips, length, heads_here, size = array.shape
    return array.transpose(0, 2, 1, 3).reshape(clips * heads_here, length, size)


def from_pairs(array, clips):
    pairs, length, size = array.shape
    return array.reshape(clips, pairs // clips, length, size).transpose(0, 2, 1, 3)


def head_forward(blocks):
    query, keys, values = blocks
    scale = query.shape[-1] ** (-0.5)
    scores = jnp.dot(query, keys.T, preferred_element_type=jnp.float32) * scale
    peak = jnp.max(scores, -1, keepdims=True)
    expo = jnp.exp(scores - peak)
    total = jnp.sum(expo, -1, keepdims=True)
    weights = (expo / total).astype(jnp.bfloat16)
    mixed = jnp.dot(weights, values, preferred_element_type=jnp.float32).astype(jnp.bfloat16)
    return (mixed, (peak + jnp.log(total))[:, 0])


def head_backward(blocks):
    query, keys, values, grad_out, logsum = blocks
    scale = query.shape[-1] ** (-0.5)
    scores = jnp.dot(query, keys.T, preferred_element_type=jnp.float32) * scale
    probs = jnp.exp(scores - logsum[:, None])
    grad_probs = jnp.dot(grad_out, values.T, preferred_element_type=jnp.float32)
    inner = jnp.sum(probs * grad_probs, -1, keepdims=True)
    grad_scores = (probs * (grad_probs - inner)).astype(jnp.bfloat16)
    grad_query = (jnp.dot(grad_scores, keys, preferred_element_type=jnp.float32) * scale).astype(
        jnp.bfloat16
    )
    grad_keys = (jnp.dot(grad_scores.T, query, preferred_element_type=jnp.float32) * scale).astype(
        jnp.bfloat16
    )
    grad_values = jnp.dot(
        probs.astype(jnp.bfloat16).T, grad_out, preferred_element_type=jnp.float32
    ).astype(jnp.bfloat16)
    return (grad_query, grad_keys, grad_values)


def run_forward(inputs, mask_rows, vectors, attn_mats, mlp_mats):
    ln1_gain, ln1_bias, b_query, b_value, b_out, ln2_gain, ln2_bias, b_fc1, b_fc2 = vectors
    w_query, w_key, w_value, w_out = attn_mats
    w_fc1, w_fc2 = mlp_mats
    clips, local_len, width = inputs.shape
    rows = inputs.reshape(clips * local_len, width).astype(jnp.float32)
    normed1, hat1, inv1 = normalize(rows, ln1_gain, ln1_bias)
    first_in = normed1.astype(jnp.bfloat16)
    head_shape = (clips, local_len, HEADS, HD)
    query = (jnp.dot(first_in, w_query, preferred_element_type=jnp.float32) + b_query).astype(
        jnp.bfloat16
    )
    keys = jnp.dot(first_in, w_key, preferred_element_type=jnp.float32).astype(jnp.bfloat16)
    values = (jnp.dot(first_in, w_value, preferred_element_type=jnp.float32) + b_value).astype(
        jnp.bfloat16
    )
    query_heads, keys_heads, values_heads = (
        lax.all_to_all(query.reshape(head_shape), "seq", split_axis=2, concat_axis=1, tiled=True),
        lax.all_to_all(keys.reshape(head_shape), "seq", split_axis=2, concat_axis=1, tiled=True),
        lax.all_to_all(values.reshape(head_shape), "seq", split_axis=2, concat_axis=1, tiled=True),
    )
    query_pairs = to_pairs(query_heads)
    keys_pairs = to_pairs(keys_heads)
    values_pairs = to_pairs(values_heads)
    mixed_pairs, logsum = lax.map(head_forward, (query_pairs, keys_pairs, values_pairs))
    mixed_tokens = lax.all_to_all(
        from_pairs(mixed_pairs, clips), "seq", split_axis=1, concat_axis=2, tiled=True
    )
    attended = mixed_tokens.reshape(clips * local_len, width)
    branch = jnp.dot(attended, w_out, preferred_element_type=jnp.float32) + b_out
    middle = rows + branch
    normed2, hat2, inv2 = normalize(middle, ln2_gain, ln2_bias)
    second_in = normed2.astype(jnp.bfloat16)
    hidden = jnp.dot(second_in, w_fc1, preferred_element_type=jnp.float32) + b_fc1
    activ = jax.nn.gelu(hidden, approximate=False).astype(jnp.bfloat16)
    final = jnp.dot(activ, w_fc2, preferred_element_type=jnp.float32) + b_fc2
    result = (middle + final) * mask_rows
    saved = (
        first_in,
        hat1,
        inv1,
        query_pairs,
        keys_pairs,
        values_pairs,
        logsum,
        attended,
        second_in,
        hat2,
        inv2,
        hidden,
        activ,
    )
    return (result, saved)


def on_device(
    inputs,
    clip_mask,
    ln1_gain,
    ln1_bias,
    w_query,
    b_query,
    w_key,
    w_value,
    b_value,
    w_out,
    b_out,
    ln2_gain,
    ln2_bias,
    w_fc1,
    b_fc1,
    w_fc2,
    b_fc2,
    cotangent,
):
    clips, local_len, width = inputs.shape
    mask_rows = jnp.repeat(clip_mask.astype(jnp.float32), local_len)[:, None]
    vectors = (ln1_gain, ln1_bias, b_query, b_value, b_out, ln2_gain, ln2_bias, b_fc1, b_fc2)
    attn_mats = (
        lax.all_gather(w_query, "fsdp", axis=0, tiled=True),
        lax.all_gather(w_key, "fsdp", axis=0, tiled=True),
        lax.all_gather(w_value, "fsdp", axis=0, tiled=True),
        lax.all_gather(w_out, "fsdp", axis=0, tiled=True),
    )
    mlp_mats = (
        lax.all_gather(w_fc1, "fsdp", axis=0, tiled=True),
        lax.all_gather(w_fc2, "fsdp", axis=0, tiled=True),
    )
    result, unused = run_forward(inputs, mask_rows, vectors, attn_mats, mlp_mats)
    output = result.reshape(clips, local_len, width).astype(jnp.bfloat16)
    attn_back = (
        lax.all_gather(w_query, "fsdp", axis=0, tiled=True),
        lax.all_gather(w_key, "fsdp", axis=0, tiled=True),
        lax.all_gather(w_value, "fsdp", axis=0, tiled=True),
        lax.all_gather(w_out, "fsdp", axis=0, tiled=True),
    )
    mlp_back = (
        lax.all_gather(w_fc1, "fsdp", axis=0, tiled=True),
        lax.all_gather(w_fc2, "fsdp", axis=0, tiled=True),
    )
    full_query, full_key, full_value, full_out = attn_back
    full_fc1, full_fc2 = mlp_back
    unused_result, saved = run_forward(inputs, mask_rows, vectors, attn_back, mlp_back)
    (
        first_in,
        hat1,
        inv1,
        query_pairs,
        keys_pairs,
        values_pairs,
        logsum,
        attended,
        second_in,
        hat2,
        inv2,
        hidden,
        activ,
    ) = saved
    grad_rows = cotangent.reshape(clips * local_len, width).astype(jnp.float32) * mask_rows
    grad_low = grad_rows.astype(jnp.bfloat16)
    grad_b_fc2 = jnp.sum(grad_rows, 0)
    grad_w_fc2 = jnp.dot(activ.T, grad_low, preferred_element_type=jnp.float32)
    grad_activ = jnp.dot(grad_low, full_fc2.T, preferred_element_type=jnp.float32)
    unused_gelu, gelu_pull = jax.vjp(lambda value: jax.nn.gelu(value, approximate=False), hidden)
    grad_hidden = gelu_pull(grad_activ)[0].astype(jnp.bfloat16)
    grad_w_fc1 = jnp.dot(second_in.T, grad_hidden, preferred_element_type=jnp.float32)
    grad_b_fc1 = jnp.sum(grad_hidden.astype(jnp.float32), 0)
    grad_second = jnp.dot(grad_hidden, full_fc1.T, preferred_element_type=jnp.float32)
    grad_ln2_gain = jnp.sum(grad_second * hat2, 0)
    grad_ln2_bias = jnp.sum(grad_second, 0)
    grad_middle = grad_rows + norm_grad(grad_second, hat2, inv2, ln2_gain)
    grad_branch = grad_middle.astype(jnp.bfloat16)
    grad_w_out = jnp.dot(attended.T, grad_branch, preferred_element_type=jnp.float32)
    grad_b_out = jnp.sum(grad_branch.astype(jnp.float32), 0)
    grad_mixed = jnp.dot(grad_branch, full_out.T, preferred_element_type=jnp.float32).astype(
        jnp.bfloat16
    )
    grad_mixed_heads = lax.all_to_all(
        grad_mixed.reshape(clips, local_len, HEADS, HD),
        "seq",
        split_axis=2,
        concat_axis=1,
        tiled=True,
    )
    grad_q_pairs, grad_k_pairs, grad_v_pairs = lax.map(
        head_backward, (query_pairs, keys_pairs, values_pairs, to_pairs(grad_mixed_heads), logsum)
    )
    grad_query, grad_keys, grad_values = (
        lax.all_to_all(
            from_pairs(grad_q_pairs, clips), "seq", split_axis=1, concat_axis=2, tiled=True
        ),
        lax.all_to_all(
            from_pairs(grad_k_pairs, clips), "seq", split_axis=1, concat_axis=2, tiled=True
        ),
        lax.all_to_all(
            from_pairs(grad_v_pairs, clips), "seq", split_axis=1, concat_axis=2, tiled=True
        ),
    )
    grad_query = grad_query.reshape(clips * local_len, width)
    grad_keys = grad_keys.reshape(clips * local_len, width)
    grad_values = grad_values.reshape(clips * local_len, width)
    grad_w_query = jnp.dot(first_in.T, grad_query, preferred_element_type=jnp.float32)
    grad_w_key = jnp.dot(first_in.T, grad_keys, preferred_element_type=jnp.float32)
    grad_w_value = jnp.dot(first_in.T, grad_values, preferred_element_type=jnp.float32)
    grad_b_query = jnp.sum(grad_query.astype(jnp.float32), 0)
    grad_b_value = jnp.sum(grad_values.astype(jnp.float32), 0)
    grad_first = (
        jnp.dot(grad_query, full_query.T, preferred_element_type=jnp.float32)
        + jnp.dot(grad_keys, full_key.T, preferred_element_type=jnp.float32)
        + jnp.dot(grad_values, full_value.T, preferred_element_type=jnp.float32)
    )
    grad_ln1_gain = jnp.sum(grad_first * hat1, 0)
    grad_ln1_bias = jnp.sum(grad_first, 0)
    grad_inputs = grad_middle + norm_grad(grad_first, hat1, inv1, ln1_gain)
    grad_inputs = grad_inputs.reshape(clips, local_len, width)
    all_grads = (
        grad_ln1_gain,
        grad_ln1_bias,
        grad_w_query,
        grad_b_query,
        grad_w_key,
        grad_w_value,
        grad_b_value,
        grad_w_out,
        grad_b_out,
        grad_ln2_gain,
        grad_ln2_bias,
        grad_w_fc1,
        grad_b_fc1,
        grad_w_fc2,
        grad_b_fc2,
    )
    owned = (
        lax.psum_scatter(all_grads[0], ("fsdp", "seq"), scatter_dimension=0, tiled=True),
        lax.psum_scatter(all_grads[1], ("fsdp", "seq"), scatter_dimension=0, tiled=True),
        lax.psum_scatter(all_grads[2], ("fsdp", "seq"), scatter_dimension=0, tiled=True),
        lax.psum_scatter(all_grads[3], ("fsdp", "seq"), scatter_dimension=0, tiled=True),
        lax.psum_scatter(all_grads[4], ("fsdp", "seq"), scatter_dimension=0, tiled=True),
        lax.psum_scatter(all_grads[5], ("fsdp", "seq"), scatter_dimension=0, tiled=True),
        lax.psum_scatter(all_grads[6], ("fsdp", "seq"), scatter_dimension=0, tiled=True),
        lax.psum_scatter(all_grads[7], ("fsdp", "seq"), scatter_dimension=0, tiled=True),
        lax.psum_scatter(all_grads[8], ("fsdp", "seq"), scatter_dimension=0, tiled=True),
        lax.psum_scatter(all_grads[9], ("fsdp", "seq"), scatter_dimension=0, tiled=True),
        lax.psum_scatter(all_grads[10], ("fsdp", "seq"), scatter_dimension=0, tiled=True),
        lax.psum_scatter(all_grads[11], ("fsdp", "seq"), scatter_dimension=0, tiled=True),
        lax.psum_scatter(all_grads[12], ("fsdp", "seq"), scatter_dimension=0, tiled=True),
        lax.psum_scatter(all_grads[13], ("fsdp", "seq"), scatter_dimension=0, tiled=True),
        lax.psum_scatter(all_grads[14], ("fsdp", "seq"), scatter_dimension=0, tiled=True),
    )
    return (
        output,
        grad_inputs,
        owned[0],
        owned[1],
        owned[2],
        owned[3],
        owned[4],
        owned[5],
        owned[6],
        owned[7],
        owned[8],
        owned[9],
        owned[10],
        owned[11],
        owned[12],
        owned[13],
        owned[14],
    )


def solution(mesh):
    return jax.shard_map(
        on_device,
        mesh=mesh,
        in_specs=(
            P("fsdp", "seq", None),
            P("fsdp"),
            P(),
            P(),
            P("fsdp", None),
            P(),
            P("fsdp", None),
            P("fsdp", None),
            P(),
            P("fsdp", None),
            P(),
            P(),
            P(),
            P("fsdp", None),
            P(),
            P("fsdp", None),
            P(),
            P("fsdp", "seq", None),
        ),
        out_specs=(
            P("fsdp", "seq", None),
            P("fsdp", "seq", None),
            P(("fsdp", "seq")),
            P(("fsdp", "seq")),
            P(("fsdp", "seq"), None),
            P(("fsdp", "seq")),
            P(("fsdp", "seq"), None),
            P(("fsdp", "seq"), None),
            P(("fsdp", "seq")),
            P(("fsdp", "seq"), None),
            P(("fsdp", "seq")),
            P(("fsdp", "seq")),
            P(("fsdp", "seq")),
            P(("fsdp", "seq"), None),
            P(("fsdp", "seq")),
            P(("fsdp", "seq"), None),
            P(("fsdp", "seq")),
        ),
        check_vma=False,
    )
```

profile of v0, /device:TPU:0, one launch (start us, length us, event | category | flops | bytes accessed | tf_op | source)
XLA Modules:
  0.0 1689.8 jit_solution(14784483086480142402)
XLA Ops:
  13.5 27.1 %all-gather.7.cloned.1.call-done = bf16[1024,1024]{1,0:T(8,128)(2,1)} async-done(((bf16[128,1024]{1,0:T(8,128)(2,1)}), bf16[1024,1024]{1,0:T(8,128)(2,1)}) %all-gather.7.cloned.1.call-update) | async-done | bytes 2097168 | tf_op jit(solution)/shard_map/all_gather | solution.py:149
  49.5 20.9 %all-gather.9.cloned.1.call-done = bf16[1024,1024]{1,0:T(8,128)(2,1)} async-done(((bf16[128,1024]{1,0:T(8,128)(2,1)}), bf16[1024,1024]{1,0:T(8,128)(2,1)}) %all-gather.9.cloned.1.call-update) | async-done | bytes 2097168 | tf_op jit(solution)/shard_map/all_gather | solution.py:150
  79.9 20.3 %all-gather.11.cloned.1.call-done = bf16[1024,1024]{1,0:T(8,128)(2,1)} async-done(((bf16[128,1024]{1,0:T(8,128)(2,1)}), bf16[1024,1024]{1,0:T(8,128)(2,1)}) %all-gather.11.cloned.1.call-update) | async-done | bytes 2097168 | tf_op jit(solution)/shard_map/all_gather | solution.py:151
  113.1 22.1 %all-to-all-done.2 = bf16[1,392,16,64]{1,3,0,2:T(8,128)(2,1)} async-done(((bf16[1,392,16,64]{1,3,0,2:T(8,128)(2,1)}), bf16[1,392,16,64]{1,3,0,2:T(8,128)(2,1)}, u32[]{:S(2)}, u32[]{:S(2)}) %all-to-all-start.2) | async-done | bytes 802848 | tf_op jit(solution)/shard_map/all_to_all | solution.py:89
  138.7 29.4 %while.37 = (s32[]{:T(128)}, bf16[4,1568,64]{1,2,0:T(8,128)(2,1)}, f32[4,1568]{1,0:T(4,128)S(1)}, bf16[4,1568,64]{2,1,0:T(8,128)(2,1)S(1)}, bf16[4,1568,64]{2,1,...) while((s32[]{:T(128)}, bf16[4,1568,64]{1,2,0:T(8,128)(2,1)}, ...), condition=%wide.region_11.12_spmd, body=%wide.region_8.0_spmd.sunk | while | flops 651634176 | bytes 30998112 | solution.py:94
  183.5 19.4 %all-to-all-done.4 = bf16[4,2,50176]{2,1,0:T(2,128)(2,1)} async-done(((bf16[4,2,50176]{2,1,0:T(2,128)(2,1)}), bf16[4,2,50176]{2,1,0:T(2,128)(2,1)}, u32[]{:S(2)}, u32[]{:S(2)}) %all-to-all-start.4) | async-done | bytes 802848 | tf_op jit(solution)/shard_map/all_to_all | solution.py:95
  215.6 21.5 %fusion.70 = (f32[392,4096]{1,0:T(8,128)}, f32[392,4096]{1,0:T(8,128)}) fusion(f32[4096]{0:T(1024)S(1)} %copy-done.16, bf16[1024,4096]{1,0:T(8,128)(2,1)} %all-gather.15.cloned.1.call-done, f32[392,1024]{1,0:T(8,128)} %copy-done.4, f32[392]{0:T(512)S(1)} %add_rsqrt_fusion, f32[392]{0:T(512)S(1)} %broadcast_multiply_fusion.4, f32[1024]{0:T(1024)S(1)} %copy-done.45, ...), kind=kOutput, calls=%fused_computation.79 | convolution fusion | flops 3391496192 | bytes 22867008 | tf_op jit(solution)/shard_map/dot_general | solution.py:103
  242.2 11.8 convert_reduce_fusion
  274.7 34.4 %all-to-all-done.5 = bf16[1,392,16,64]{1,3,0,2:T(8,128)(2,1)} async-done(((bf16[1,392,16,64]{1,3,0,2:T(8,128)(2,1)}), bf16[1,392,16,64]{1,3,0,2:T(8,128)(2,1)}, u32[]{:S(2)}, u32[]{:S(2)}) %all-to-all-start.5) | async-done | bytes 802848 | tf_op jit(solution)/shard_map/all_to_all | solution.py:207
  315.2 131.6 %while.38 = (s32[]{:T(128)}, bf16[4,1568,64]{1,2,0:T(8,128)(2,1)}, bf16[4,1568,64]{1,2,0:T(8,128)(2,1)}, bf16[4,1568,64]{1,2,0:T(8,128)(2,1)}, bf16[4,1568,64]{2...) while((s32[]{:T(128)}, bf16[4,1568,64]{1,2,0:T(8,128)(2,1)}, ...), condition=%wide.region_18.19_spmd, body=%wide.region_16.18_spmd.sunk | while | flops 1593688576 | bytes 157126304 | solution.py:214
  324.8 10.5 multiply_convert_fusion.5
  423.6 10.5 multiply_convert_fusion.5
  457.1 21.4 %all_to_all.162 = bf16[4,2,50176]{2,1,0:T(2,128)(2,1)} all-to-all(bf16[4,2,50176]{2,1,0:T(2,128)(2,1)} %reshape.302), channel_id=1, replica_groups=mesh['fsdp'=8,'seq'=4] {'seq'}, dimensions={0} | all-to-all | bytes 1605632 | tf_op jit(solution)/shard_map/all_to_all | solution.py:218
  501.9 40.5 %all_to_all.163 = bf16[4,2,50176]{2,1,0:T(2,128)(2,1)} all-to-all(bf16[4,2,50176]{2,1,0:T(2,128)(2,1)} %reshape.304), channel_id=1, replica_groups=mesh['fsdp'=8,'seq'=4] {'seq'}, dimensions={0} | all-to-all | bytes 1605632 | tf_op jit(solution)/shard_map/all_to_all | solution.py:221
  565.8 39.4 %all_to_all.164 = bf16[4,2,50176]{2,1,0:T(2,128)(2,1)} all-to-all(bf16[4,2,50176]{2,1,0:T(2,128)(2,1)} %reshape.306), channel_id=1, replica_groups=mesh['fsdp'=8,'seq'=4] {'seq'}, dimensions={0} | all-to-all | bytes 1605632 | tf_op jit(solution)/shard_map/all_to_all | solution.py:224
  619.0 13.0 fusion.182
  632.7 15.5 fusion.83
  649.1 28.9 %while.36 = (s32[]{:T(128)}, bf16[4,1568,64]{1,2,0:T(8,128)(2,1)}, bf16[4,1568,64]{2,1,0:T(8,128)(2,1)S(1)}, bf16[4,1568,64]{2,1,0:T(8,128)(2,1)S(1)}, bf16[4,1568,64]{2,1,0:T(8,128)(2,1)}, /*index=5*/s32[]{:T(128)}) while((s32[]{:T(128)}, bf16[4,1568,64]{1,2,0:T(8,128)(2,1)}, bf16[4,1568,64]{2,1,0:T(8,128)(2,1)S(1)}, ...), condition=%wide.region_5.6_spmd, body=%wide.region_2.5_spmd.sunk | while | flops 651632576 | bytes 30954188 | solution.py:94
  690.8 33.4 %all-to-all-done.3 = bf16[4,2,50176]{2,1,0:T(2,128)(2,1)S(1)} async-done(((bf16[4,2,50176]{2,1,0:T(2,128)(2,1)}), bf16[4,2,50176]{2,1,0:T(2,128)(2,1)S(1)}, u32[]{:S(2)}, u32[]{:S(2)}) %all-to-all-start.3) | async-done | bytes 802848 | tf_op jit(solution)/shard_map/all_to_all | solution.py:95
  730.1 26.3 %fusion.137 = bf16[1,392,1024]{2,1,0:T(8,128)(2,1)} fusion(f32[392,1024]{1,0:T(8,128)S(1)} %get-tuple-element.198, bf16[4096,1024]{1,0:T(8,128)(2,1)} %all-gather.17.cloned.1.call-done, bf16[1024,4096]{1,0:T(8,128)(2,1)} %all-gather.15.cloned.1.call-done, f32[4096]{0:T(1024)S(1)} %copy-done.17, f32[]{:T(128)} %bitcast.42, f32[1024]{0:T(1024)S(1)} %copy-done.44, ...), kind=kOutput, calls=%fused_computation.189 | convolution fusion | flops 6686253056 | bytes 19217476 | tf_op jit(solution)/shard_map/dot_general | solution.py:105
  766.5 39.0 %all-reduce.9 = (f32[1024]{0:T(1024)S(1)}, f32[1024]{0:T(1024)S(1)}, f32[1024]{0:T(1024)S(1)}, f32[1024]{0:T(1024)S(1)}, f32[1024]{0:T(1024)S(1)}, /*index=5*/f3...) all-reduce(f32[1024]{0:T(1024)S(1)} %get-tuple-element.134, ...), channel_id=2, replica_groups=mesh['fsdp'=8,'seq'=4] {'fsdp','seq'}, use_global_device_ids=true, to_apply=%region_22.23.clone | all-reduce | flops 12288 | bytes 98304
  813.9 138.1 %reduce-scatter.11.cloned.1.call-done = f32[32,1024]{1,0:T(8,128)} async-done(((f32[1024,1024]{1,0:T(8,128)}), f32[32,1024]{1,0:T(8,128)}) %reduce-scatter.11.cloned.1.call-update) | async-done | bytes 131088 | tf_op jit(solution)/shard_map/reduce_scatter | solution.py:268
  952.1 365.8 %reduce-scatter.15.cloned.1.call-done = f32[32,4096]{1,0:T(8,128)} async-done(((f32[1024,4096]{1,0:T(8,128)}), f32[32,4096]{1,0:T(8,128)}) %reduce-scatter.15.cloned.1.call-update) | async-done | bytes 524304 | tf_op jit(solution)/shard_map/reduce_scatter | solution.py:274
  1317.9 364.9 %reduce-scatter.17.cloned.1.call-done = f32[128,1024]{1,0:T(8,128)} async-done(((f32[4096,1024]{1,0:T(8,128)}), f32[128,1024]{1,0:T(8,128)}) %reduce-scatter.17.cloned.1.call-update) | async-done | bytes 524304 | tf_op jit(solution)/shard_map/reduce_scatter | solution.py:276
  (292 shorter events, 378.2 us)
Async XLA Ops:
  7.2 33.4 %all-gather.7.cloned.1.call-start = ((), (), s32[]{:S(2)}) async-start(), calls=%async_computation.15 | async-start | bytes 2359296 | tf_op jit(solution)/shard_map/all_gather | solution.py:149
  7.9 62.4 %all-gather.9.cloned.1.call-start = ((), (), s32[]{:S(2)}) async-start(), calls=%async_computation.16 | async-start | bytes 2359296 | tf_op jit(solution)/shard_map/all_gather | solution.py:150
  8.7 91.5 %all-gather.11.cloned.1.call-start = ((), (), s32[]{:S(2)}) async-start(), calls=%async_computation.17 | async-start | bytes 2359296 | tf_op jit(solution)/shard_map/all_gather | solution.py:151
  9.4 201.4 %all-gather.13.cloned.1.call-start = ((), (), s32[]{:S(2)}) async-start(), calls=%async_computation.18 | async-start | bytes 2359296 | tf_op jit(solution)/shard_map/all_gather | solution.py:152
  10.0 205.6 %all-gather.15.cloned.1.call-start = ((), (), s32[]{:S(2)}) async-start(), calls=%async_computation.19 | async-start | bytes 9437184 | tf_op jit(solution)/shard_map/all_gather | solution.py:155
  11.9 88.3 %copy-start.18 = (f32[392]{0:T(512)}, f32[392]{0:T(512)S(1)}, u32[]{:S(2)}) copy-start(f32[392]{0:T(512)S(1)} %broadcast_multiply_fusion.6) | copy-start | bytes 4708
  13.4 86.8 %copy-start.25 = (f32[392]{0:T(512)}, f32[392]{0:T(512)S(1)}, u32[]{:S(2)}) copy-start(f32[392]{0:T(512)S(1)} %add_rsqrt_fusion.2) | copy-start | bytes 4708
  13.4 56.9 %copy-start.2 = (bf16[1,392,1024]{2,1,0:T(8,128)(2,1)S(1)}, bf16[1,392,1024]{2,1,0:T(8,128)(2,1)}, u32[]{:S(2)}) copy-start(bf16[1,392,1024]{2,1,0:T(8,128)(2,1)} %param.24) | copy-start | bytes 2408452
  13.4 56.9 %copy-start.30 = (f32[1024]{0:T(1024)S(1)}, f32[1024]{0:T(1024)}, u32[]{:S(2)}) copy-start(f32[1024]{0:T(1024)} %param.26) | copy-start | bytes 12292
  13.4 56.9 %copy-start.42 = (f32[1024]{0:T(1024)S(1)}, f32[1024]{0:T(1024)}, u32[]{:S(2)}) copy-start(f32[1024]{0:T(1024)} %param.27) | copy-start | bytes 12292
  44.8 30.8 %all-to-all-start = ((bf16[1,392,16,64]{1,3,0,2:T(8,128)(2,1)}), bf16[1,392,16,64]{1,3,0,2:T(8,128)(2,1)S(1)}, u32[]{:S(2)}, u32[]{:S(2)}) async-start(bf16[1,392,16,64]{1,3,0,2:T(8,128)(2,1)} %bitcast.17), calls=%async_computation | async-start | bytes 2097152 | tf_op jit(solution)/shard_map/all_to_all | solution.py:87
  49.5 50.7 %copy-start.41 = (f32[1024]{0:T(1024)S(1)}, f32[1024]{0:T(1024)}, u32[]{:S(2)}) copy-start(f32[1024]{0:T(1024)} %param.32) | copy-start | bytes 12292
  75.6 29.7 %all-to-all-start.1 = ((bf16[1,392,16,64]{1,3,0,2:T(8,128)(2,1)}), bf16[1,392,16,64]{1,3,0,2:T(8,128)(2,1)}, u32[]{:S(2)}, u32[]{:S(2)}) async-start(bf16[1,392,16,64]{1,3,0,2:T(8,128)(2,1)} %bitcast.24), calls=%async_computation.1 | async-start | bytes 2097152 | tf_op jit(solution)/shard_map/all_to_all | solution.py:88
  105.3 29.8 %all-to-all-start.2 = ((bf16[1,392,16,64]{1,3,0,2:T(8,128)(2,1)}), bf16[1,392,16,64]{1,3,0,2:T(8,128)(2,1)}, u32[]{:S(2)}, u32[]{:S(2)}) async-start(bf16[1,392,16,64]{1,3,0,2:T(8,128)(2,1)} %bitcast.31), calls=%async_computation.2 | async-start | bytes 2097152 | tf_op jit(solution)/shard_map/all_to_all | solution.py:89
  109.6 132.6 %all-gather.17.cloned.1.call-start = ((), (), s32[]{:S(2)}) async-start(), calls=%async_computation.20 | async-start | bytes 9437184 | tf_op jit(solution)/shard_map/all_gather | solution.py:156
  178.4 24.5 %all-to-all-start.4 = ((bf16[4,2,50176]{2,1,0:T(2,128)(2,1)}), bf16[4,2,50176]{2,1,0:T(2,128)(2,1)}, u32[]{:S(2)}, u32[]{:S(2)}) async-start(bf16[4,2,50176]{2,1,0:T(2,128)(2,1)} %reshape.300), calls=%async_computation.4 | async-start | bytes 1605632 | tf_op jit(solution)/shard_map/all_to_all | solution.py:95
  265.1 44.0 %all-to-all-start.5 = ((bf16[1,392,16,64]{1,3,0,2:T(8,128)(2,1)}), bf16[1,392,16,64]{1,3,0,2:T(8,128)(2,1)}, u32[]{:S(2)}, u32[]{:S(2)}) async-start(bf16[1,392,16,64]{1,3,0,2:T(8,128)(2,1)} %bitcast.308), calls=%async_computation.5 | async-start | bytes 2097152 | tf_op jit(solution)/shard_map/all_to_all | solution.py:207
  269.7 544.2 %reduce-scatter.13.cloned.1.call-start = ((), (), s32[]{:S(2)}) async-start(), calls=%async_computation.24 | async-start | bytes 4325376 | tf_op jit(solution)/shard_map/reduce_scatter | solution.py:270
  274.7 539.2 %reduce-scatter.7.cloned.1.call-start = ((), (), s32[]{:S(2)}) async-start(), calls=%async_computation.21 | async-start | bytes 4325376 | tf_op jit(solution)/shard_map/reduce_scatter | solution.py:265
  491.5 322.4 %reduce-scatter.9.cloned.1.call-start = ((), (), s32[]{:S(2)}) async-start(), calls=%async_computation.22 | async-start | bytes 4325376 | tf_op jit(solution)/shard_map/reduce_scatter | solution.py:267
  555.5 396.6 %reduce-scatter.11.cloned.1.call-start = ((), (), s32[]{:S(2)}) async-start(), calls=%async_computation.23 | async-start | bytes 4325376 | tf_op jit(solution)/shard_map/reduce_scatter | solution.py:268
  618.3 699.6 %reduce-scatter.15.cloned.1.call-start = ((), (), s32[]{:S(2)}) async-start(), calls=%async_computation.25 | async-start | bytes 17301504 | tf_op jit(solution)/shard_map/reduce_scatter | solution.py:274
  632.0 1050.8 %reduce-scatter.17.cloned.1.call-start = ((), (), s32[]{:S(2)}) async-start(), calls=%async_computation.26 | async-start | bytes 17301504 | tf_op jit(solution)/shard_map/reduce_scatter | solution.py:276
  686.8 37.4 %all-to-all-start.3 = ((bf16[4,2,50176]{2,1,0:T(2,128)(2,1)}), bf16[4,2,50176]{2,1,0:T(2,128)(2,1)S(1)}, u32[]{:S(2)}, u32[]{:S(2)}) async-start(bf16[4,2,50176]{2,1,0:T(2,128)(2,1)} %reshape.298), calls=%async_computation.3 | async-start | bytes 1605632 | tf_op jit(solution)/shard_map/all_to_all | solution.py:95
  (49 other events, 578.2 us)
Sparse Core Ops, SparseCore 0:
  9.9 30.5 all-gather.6
  42.4 27.8 all-gather.8
  72.2 27.8 all-gather.10
  101.9 27.8 all-gather.12
  131.6 54.4 all-gather.14
  187.8 54.3 all-gather.16
  274.8 153.5 reduce-scatter.12
  491.7 155.6 reduce-scatter.6
  650.2 152.9 reduce-scatter.8
  805.8 146.1 reduce-scatter.10
  954.9 362.8 reduce-scatter.14
  1320.6 362.1 reduce-scatter.16
where the time goes:
time: 1700 us; the launch traced here: 1690 us
  waiting for transfers between devices  1060 us (62%)
  matrix products  265 us (16%)
  blocking collectives  140 us (8%)
  local copies, waits for them, and re-layouts  119 us (7%)
  other arithmetic  65.8 us (4%)
  starting transfers between devices  26.8 us (2%)
    reduce_scatter x1, waiting for transfers between devices, on_device(): lax.psum_scatter(all_grads[11], ('fsdp', 'seq'), scatter_dimension=0, til...  366 us
    reduce_scatter x1, waiting for transfers between devices, on_device(): lax.psum_scatter(all_grads[13], ('fsdp', 'seq'), scatter_dimension=0, til...  365 us
    reduce_scatter x1, waiting for transfers between devices, on_device(): lax.psum_scatter(all_grads[5], ('fsdp', 'seq'), scatter_dimension=0, tile...  138 us
    unnamed x118, local copies, waits for them, and re-layouts  58 us
    all_to_all x2, waiting for transfers between devices, run_forward(): lax.all_to_all(from_pairs(mixed_pairs, clips), 'seq', split_axis=1, conca...  52.8 us
    convert_element_type x4, other arithmetic, head_backward(): grad_scores = (probs * (grad_probs - inner)).astype(jnp.bfloat16)  41.9 us
    all_to_all x1, blocking collectives, on_device(): lax.all_to_all(from_pairs(grad_k_pairs, clips), 'seq', split_axis=1, conc...  40.5 us
    all_to_all x1, blocking collectives, on_device(): lax.all_to_all(from_pairs(grad_v_pairs, clips), 'seq', split_axis=1, conc...  39.4 us
  transfers between devices with their start and end apart: 18, of which 13 were waited for; matrix products, arithmetic and copies ran while one was open for 25% of the time, Pallas kernels for 0%

commit v1 on v0

--- a/solution.py
+++ b/solution.py
@@ -6,6 +6,39 @@
 HEADS = 16
 HD = 64
 EPSILON = 1e-06
+
+
+def hold_row(content, on_dim, x0):
+    new = content.shape
+    formed = content.reshape(*new[:on_dim], x0, new[on_dim] // x0, *new[on_dim + 1 :])
+    return jnp.moveaxis(formed, on_dim, 0)
+
+
+def _pair_ratios(sheet, ndim_at):
+    sheet = jnp.moveaxis(sheet, 0, ndim_at)
+    outcome_arr = sheet.shape
+    return sheet.reshape(
+        *outcome_arr[:ndim_at],
+        outcome_arr[ndim_at] * outcome_arr[ndim_at + 1],
+        *outcome_arr[ndim_at + 2 :]
+    )
+
+
+def arrays_divide(load, dev_axis, s0, q_in):
+    upper, carry_out = (jax.lax.psum(1, dev_axis), jax.lax.axis_index(dev_axis))
+    odd = hold_row(load, s0, upper)
+    queue = [odd[carry_out]]
+    for ix in [*range(1, upper)]:
+        frame_out = odd[(carry_out + ix) % upper]
+        queue.append(
+            jax.lax.ppermute(
+                frame_out,
+                axis_name=dev_axis,
+                perm=[(hop_no, (hop_no + ix) % upper) for hop_no in range(upper)],
+            )
+        )
+    odd = jnp.stack(queue)[(carry_out - jnp.arange(upper)) % upper]
+    return _pair_ratios(odd, q_in)
 
 
 def normalize(rows, gain, shift):
@@ -204,12 +237,8 @@
     grad_mixed = jnp.dot(grad_branch, full_out.T, preferred_element_type=jnp.float32).astype(
         jnp.bfloat16
     )
-    grad_mixed_heads = lax.all_to_all(
-        grad_mixed.reshape(clips, local_len, HEADS, HD),
-        "seq",
-        split_axis=2,
-        concat_axis=1,
-        tiled=True,
+    grad_mixed_heads = arrays_divide(
+        grad_mixed.reshape(clips, local_len, HEADS, HD), "seq", s0=2, q_in=1
     )
     grad_q_pairs, grad_k_pairs, grad_v_pairs = lax.map(
         head_backward, (query_pairs, keys_pairs, values_pairs, to_pairs(grad_mixed_heads), logsum)

time: 1700 us -> 1700 us (level)
    all_to_all x1 -> x0, waiting for transfers between devices: 34.4 us -> none  [on_device(): lax.all_to_all(grad_mixed.reshape(clips, local_len, HEADS, HD), 'seq', sp...]
    ppermute x0 -> x3, waiting for transfers between devices: none -> 25.6 us  [arrays_divide(): jax.lax.ppermute(frame_out, axis_name=dev_axis, perm=[(hop_no, (hop_no +...]
    unnamed x118 -> x116, local copies, waits for them, and re-layouts: 58 us -> 58 us
  transfers between devices with their start and end apart: 18 -> 20, of which waited for: 13 -> 14; matrix products, arithmetic and copies ran while one was open for 25% -> 25% of each run, Pallas kernels for 0% -> 0%
where the time goes in v1:
time: 1700 us
  waiting for transfers between devices  1050 us (62%)
  matrix products  265 us (16%)
  blocking collectives  146 us (9%)
  local copies, waits for them, and re-layouts  129 us (8%)
  other arithmetic  69.3 us (4%)
  starting transfers between devices  26.4 us (2%)
    reduce_scatter x1, waiting for transfers between devices, on_device(): lax.psum_scatter(all_grads[11], ('fsdp', 'seq'), scatter_dimension=0, til...  366 us
    reduce_scatter x1, waiting for transfers between devices, on_device(): lax.psum_scatter(all_grads[13], ('fsdp', 'seq'), scatter_dimension=0, til...  365 us
    reduce_scatter x1, waiting for transfers between devices, on_device(): lax.psum_scatter(all_grads[5], ('fsdp', 'seq'), scatter_dimension=0, tile...  135 us
    unnamed x116, local copies, waits for them, and re-layouts  58 us
    all_to_all x2, waiting for transfers between devices, run_forward(): lax.all_to_all(from_pairs(mixed_pairs, clips), 'seq', split_axis=1, conca...  53.2 us
    convert_element_type x4, other arithmetic, head_backward(): grad_scores = (probs * (grad_probs - inner)).astype(jnp.bfloat16)  41.9 us
    all_to_all x1, blocking collectives, on_device(): lax.all_to_all(from_pairs(grad_k_pairs, clips), 'seq', split_axis=1, conc...  41.5 us
    all_to_all x1, blocking collectives, on_device(): lax.all_to_all(from_pairs(grad_v_pairs, clips), 'seq', split_axis=1, conc...  40.3 us
  transfers between devices with their start and end apart: 20, of which 14 were waited for; matrix products, arithmetic and copies ran while one was open for 25% of the time, Pallas kernels for 0%

profile of v1, /device:TPU:0, one launch (start us, length us, event | category | flops | bytes accessed | tf_op | source)
XLA Modules:
  0.0 1696.5 jit_solution(529424338691992760)
XLA Ops:
  13.5 27.1 %all-gather.7.cloned.1.call-done = bf16[1024,1024]{1,0:T(8,128)(2,1)} async-done(((bf16[128,1024]{1,0:T(8,128)(2,1)}), bf16[1024,1024]{1,0:T(8,128)(2,1)}) %all-gather.7.cloned.1.call-update) | async-done | bytes 2097168 | tf_op jit(solution)/shard_map/all_gather | solution.py:182
  49.5 20.9 %all-gather.9.cloned.1.call-done = bf16[1024,1024]{1,0:T(8,128)(2,1)} async-done(((bf16[128,1024]{1,0:T(8,128)(2,1)}), bf16[1024,1024]{1,0:T(8,128)(2,1)}) %all-gather.9.cloned.1.call-update) | async-done | bytes 2097168 | tf_op jit(solution)/shard_map/all_gather | solution.py:183
  79.8 20.3 %all-gather.11.cloned.1.call-done = bf16[1024,1024]{1,0:T(8,128)(2,1)} async-done(((bf16[128,1024]{1,0:T(8,128)(2,1)}), bf16[1024,1024]{1,0:T(8,128)(2,1)}) %all-gather.11.cloned.1.call-update) | async-done | bytes 2097168 | tf_op jit(solution)/shard_map/all_gather | solution.py:184
  113.1 22.1 %all-to-all-done.2 = bf16[1,392,16,64]{1,3,0,2:T(8,128)(2,1)} async-done(((bf16[1,392,16,64]{1,3,0,2:T(8,128)(2,1)}), bf16[1,392,16,64]{1,3,0,2:T(8,128)(2,1)}, u32[]{:S(2)}, u32[]{:S(2)}) %all-to-all-start.2) | async-done | bytes 802848 | tf_op jit(solution)/shard_map/all_to_all | solution.py:122
  138.7 29.5 %while.37 = (s32[]{:T(128)}, bf16[4,1568,64]{1,2,0:T(8,128)(2,1)}, f32[4,1568]{1,0:T(4,128)S(1)}, bf16[4,1568,64]{2,1,0:T(8,128)(2,1)S(1)}, bf16[4,1568,64]{2,1,...) while((s32[]{:T(128)}, bf16[4,1568,64]{1,2,0:T(8,128)(2,1)}, ...), condition=%wide.region_11.12_spmd, body=%wide.region_8.0_spmd.sunk | while | flops 651634176 | bytes 30998112 | solution.py:127
  183.7 19.1 %all-to-all-done.4 = bf16[4,2,50176]{2,1,0:T(2,128)(2,1)} async-done(((bf16[4,2,50176]{2,1,0:T(2,128)(2,1)}), bf16[4,2,50176]{2,1,0:T(2,128)(2,1)}, u32[]{:S(2)}, u32[]{:S(2)}) %all-to-all-start.4) | async-done | bytes 802848 | tf_op jit(solution)/shard_map/all_to_all | solution.py:128
  215.5 21.5 %fusion.70 = (f32[392,4096]{1,0:T(8,128)}, f32[392,4096]{1,0:T(8,128)}) fusion(f32[4096]{0:T(1024)S(1)} %copy-done.15, bf16[1024,4096]{1,0:T(8,128)(2,1)} %all-gather.15.cloned.1.call-done, f32[392,1024]{1,0:T(8,128)} %copy-done.4, f32[392]{0:T(512)S(1)} %add_rsqrt_fusion, f32[392]{0:T(512)S(1)} %broadcast_multiply_fusion.4, f32[1024]{0:T(1024)S(1)} %copy-done.44, ...), kind=kOutput, calls=%fused_computation.80 | convolution fusion | flops 3391496192 | bytes 22867008 | tf_op jit(solution)/shard_map/dot_general | solution.py:136
  242.2 11.8 convert_reduce_fusion
  277.6 24.6 %collective-permute-done.1 = bf16[1,392,4,64]{1,3,2,0:T(8,128)(2,1)} collective-permute-done((bf16[1,392,4,64]{1,3,2,0:T(8,128)(2,1)}, bf16[1,392,4,64]{1,3,2,0:T(8,128)(2,1)}, u32[]{:S(2)}, u32[]{:S(2)}) %collective-permute-start.1) | collective-permute-done | bytes 200736 | tf_op jit(solution)/shard_map/ppermute | solution.py:34
  316.9 131.2 %while.38 = (s32[]{:T(128)}, bf16[4,1568,64]{1,2,0:T(8,128)(2,1)}, bf16[4,1568,64]{1,2,0:T(8,128)(2,1)}, bf16[4,1568,64]{1,2,0:T(8,128)(2,1)}, bf16[4,1568,64]{2...) while((s32[]{:T(128)}, bf16[4,1568,64]{1,2,0:T(8,128)(2,1)}, ...), condition=%wide.region_18.19_spmd, body=%wide.region_16.18_spmd.sunk | while | flops 1593688576 | bytes 156749472 | solution.py:243
  392.1 10.5 multiply_convert_fusion.5
  424.9 10.5 multiply_convert_fusion.5
  458.4 25.4 %all_to_all.144 = bf16[4,2,50176]{2,1,0:T(2,128)(2,1)} all-to-all(bf16[4,2,50176]{2,1,0:T(2,128)(2,1)} %reshape.365), channel_id=1, replica_groups=mesh['fsdp'=8,'seq'=4] {'seq'}, dimensions={0} | all-to-all | bytes 1605632 | tf_op jit(solution)/shard_map/all_to_all | solution.py:247
  507.4 41.5 %all_to_all.145 = bf16[4,2,50176]{2,1,0:T(2,128)(2,1)} all-to-all(bf16[4,2,50176]{2,1,0:T(2,128)(2,1)} %reshape.367), channel_id=1, replica_groups=mesh['fsdp'=8,'seq'=4] {'seq'}, dimensions={0} | all-to-all | bytes 1605632 | tf_op jit(solution)/shard_map/all_to_all | solution.py:250
  572.3 40.3 %all_to_all.146 = bf16[4,2,50176]{2,1,0:T(2,128)(2,1)} all-to-all(bf16[4,2,50176]{2,1,0:T(2,128)(2,1)} %reshape.369), channel_id=1, replica_groups=mesh['fsdp'=8,'seq'=4] {'seq'}, dimensions={0} | all-to-all | bytes 1605632 | tf_op jit(solution)/shard_map/all_to_all | solution.py:253
  626.4 13.0 fusion.184
  640.1 15.5 fusion.83
  656.6 28.9 %while.36 = (s32[]{:T(128)}, bf16[4,1568,64]{1,2,0:T(8,128)(2,1)}, bf16[4,1568,64]{2,1,0:T(8,128)(2,1)S(1)}, bf16[4,1568,64]{2,1,0:T(8,128)(2,1)S(1)}, bf16[4,1568,64]{2,1,0:T(8,128)(2,1)}, /*index=5*/s32[]{:T(128)}) while((s32[]{:T(128)}, bf16[4,1568,64]{1,2,0:T(8,128)(2,1)}, bf16[4,1568,64]{2,1,0:T(8,128)(2,1)S(1)}, ...), condition=%wide.region_5.6_spmd, body=%wide.region_2.5_spmd.sunk | while | flops 651632576 | bytes 30954188 | solution.py:127
  698.1 34.1 %all-to-all-done.3 = bf16[4,2,50176]{2,1,0:T(2,128)(2,1)S(1)} async-done(((bf16[4,2,50176]{2,1,0:T(2,128)(2,1)}), bf16[4,2,50176]{2,1,0:T(2,128)(2,1)S(1)}, u32[]{:S(2)}, u32[]{:S(2)}) %all-to-all-start.3) | async-done | bytes 802848 | tf_op jit(solution)/shard_map/all_to_all | solution.py:128
  739.5 26.3 %fusion.137 = bf16[1,392,1024]{2,1,0:T(8,128)(2,1)} fusion(f32[392,1024]{1,0:T(8,128)S(1)} %get-tuple-element.220, bf16[4096,1024]{1,0:T(8,128)(2,1)} %all-gather.17.cloned.1.call-done, bf16[1024,4096]{1,0:T(8,128)(2,1)} %all-gather.15.cloned.1.call-done, f32[4096]{0:T(1024)S(1)} %copy-done.16, f32[]{:T(128)} %bitcast.42, f32[1024]{0:T(1024)S(1)} %copy-done.43, ...), kind=kOutput, calls=%fused_computation.190 | convolution fusion | flops 6686253056 | bytes 19217476 | tf_op jit(solution)/shard_map/dot_general | solution.py:138
  777.3 38.4 %all-reduce.9 = (f32[1024]{0:T(1024)S(1)}, f32[1024]{0:T(1024)S(1)}, f32[1024]{0:T(1024)S(1)}, f32[1024]{0:T(1024)S(1)}, f32[1024]{0:T(1024)S(1)}, /*index=5*/f3...) all-reduce(f32[1024]{0:T(1024)S(1)} %get-tuple-element.152, ...), channel_id=2, replica_groups=mesh['fsdp'=8,'seq'=4] {'fsdp','seq'}, use_global_device_ids=true, to_apply=%region_22.23.clone | all-reduce | flops 12288 | bytes 98304
  824.1 134.6 %reduce-scatter.11.cloned.1.call-done = f32[32,1024]{1,0:T(8,128)} async-done(((f32[1024,1024]{1,0:T(8,128)}), f32[32,1024]{1,0:T(8,128)}) %reduce-scatter.11.cloned.1.call-update) | async-done | bytes 131088 | tf_op jit(solution)/shard_map/reduce_scatter | solution.py:297
  958.6 365.9 %reduce-scatter.15.cloned.1.call-done = f32[32,4096]{1,0:T(8,128)} async-done(((f32[1024,4096]{1,0:T(8,128)}), f32[32,4096]{1,0:T(8,128)}) %reduce-scatter.15.cloned.1.call-update) | async-done | bytes 524304 | tf_op jit(solution)/shard_map/reduce_scatter | solution.py:303
  1324.6 364.9 %reduce-scatter.17.cloned.1.call-done = f32[128,1024]{1,0:T(8,128)} async-done(((f32[4096,1024]{1,0:T(8,128)}), f32[128,1024]{1,0:T(8,128)}) %reduce-scatter.17.cloned.1.call-update) | async-done | bytes 524304 | tf_op jit(solution)/shard_map/reduce_scatter | solution.py:305
  (300 shorter events, 392.5 us)
Async XLA Ops:
  7.2 33.4 %all-gather.7.cloned.1.call-start = ((), (), s32[]{:S(2)}) async-start(), calls=%async_computation.14 | async-start | bytes 2359296 | tf_op jit(solution)/shard_map/all_gather | solution.py:182
  7.9 62.4 %all-gather.9.cloned.1.call-start = ((), (), s32[]{:S(2)}) async-start(), calls=%async_computation.15 | async-start | bytes 2359296 | tf_op jit(solution)/shard_map/all_gather | solution.py:183
  8.7 91.5 %all-gather.11.cloned.1.call-start = ((), (), s32[]{:S(2)}) async-start(), calls=%async_computation.16 | async-start | bytes 2359296 | tf_op jit(solution)/shard_map/all_gather | solution.py:184
  9.4 201.3 %all-gather.13.cloned.1.call-start = ((), (), s32[]{:S(2)}) async-start(), calls=%async_computation.17 | async-start | bytes 2359296 | tf_op jit(solution)/shard_map/all_gather | solution.py:185
  10.0 205.5 %all-gather.15.cloned.1.call-start = ((), (), s32[]{:S(2)}) async-start(), calls=%async_computation.18 | async-start | bytes 9437184 | tf_op jit(solution)/shard_map/all_gather | solution.py:188
  11.9 88.3 %copy-start.17 = (f32[392]{0:T(512)}, f32[392]{0:T(512)S(1)}, u32[]{:S(2)}) copy-start(f32[392]{0:T(512)S(1)} %broadcast_multiply_fusion.6) | copy-start | bytes 4708
  13.4 86.8 %copy-start.24 = (f32[392]{0:T(512)}, f32[392]{0:T(512)S(1)}, u32[]{:S(2)}) copy-start(f32[392]{0:T(512)S(1)} %add_rsqrt_fusion.2) | copy-start | bytes 4708
  13.4 56.9 %copy-start.2 = (bf16[1,392,1024]{2,1,0:T(8,128)(2,1)S(1)}, bf16[1,392,1024]{2,1,0:T(8,128)(2,1)}, u32[]{:S(2)}) copy-start(bf16[1,392,1024]{2,1,0:T(8,128)(2,1)} %param.24) | copy-start | bytes 2408452
  13.4 56.9 %copy-start.29 = (f32[1024]{0:T(1024)S(1)}, f32[1024]{0:T(1024)}, u32[]{:S(2)}) copy-start(f32[1024]{0:T(1024)} %param.26) | copy-start | bytes 12292
  44.8 30.8 %all-to-all-start = ((bf16[1,392,16,64]{1,3,0,2:T(8,128)(2,1)}), bf16[1,392,16,64]{1,3,0,2:T(8,128)(2,1)S(1)}, u32[]{:S(2)}, u32[]{:S(2)}) async-start(bf16[1,392,16,64]{1,3,0,2:T(8,128)(2,1)} %bitcast.17), calls=%async_computation | async-start | bytes 2097152 | tf_op jit(solution)/shard_map/all_to_all | solution.py:120
  75.6 29.7 %all-to-all-start.1 = ((bf16[1,392,16,64]{1,3,0,2:T(8,128)(2,1)}), bf16[1,392,16,64]{1,3,0,2:T(8,128)(2,1)}, u32[]{:S(2)}, u32[]{:S(2)}) async-start(bf16[1,392,16,64]{1,3,0,2:T(8,128)(2,1)} %bitcast.24), calls=%async_computation.1 | async-start | bytes 2097152 | tf_op jit(solution)/shard_map/all_to_all | solution.py:121
  105.4 29.8 %all-to-all-start.2 = ((bf16[1,392,16,64]{1,3,0,2:T(8,128)(2,1)}), bf16[1,392,16,64]{1,3,0,2:T(8,128)(2,1)}, u32[]{:S(2)}, u32[]{:S(2)}) async-start(bf16[1,392,16,64]{1,3,0,2:T(8,128)(2,1)} %bitcast.31), calls=%async_computation.2 | async-start | bytes 2097152 | tf_op jit(solution)/shard_map/all_to_all | solution.py:122
  109.6 132.6 %all-gather.17.cloned.1.call-start = ((), (), s32[]{:S(2)}) async-start(), calls=%async_computation.19 | async-start | bytes 9437184 | tf_op jit(solution)/shard_map/all_gather | solution.py:189
  178.5 24.3 %all-to-all-start.4 = ((bf16[4,2,50176]{2,1,0:T(2,128)(2,1)}), bf16[4,2,50176]{2,1,0:T(2,128)(2,1)}, u32[]{:S(2)}, u32[]{:S(2)}) async-start(bf16[4,2,50176]{2,1,0:T(2,128)(2,1)} %reshape.363), calls=%async_computation.4 | async-start | bytes 1605632 | tf_op jit(solution)/shard_map/all_to_all | solution.py:128
  182.7 641.4 %reduce-scatter.13.cloned.1.call-start = ((), (), s32[]{:S(2)}) async-start(), calls=%async_computation.23 | async-start | bytes 4325376 | tf_op jit(solution)/shard_map/reduce_scatter | solution.py:299
  267.2 10.4 collective-permute-start.2
  270.5 31.7 %collective-permute-start.1 = (bf16[1,392,4,64]{1,3,2,0:T(8,128)(2,1)}, bf16[1,392,4,64]{1,3,2,0:T(8,128)(2,1)}, u32[]{:S(2)}, u32[]{:S(2)}) collective-permute-start(bf16[1,392,4,64]{1,3,2,0:T(8,128)(2,1)} %get-tuple-element.217), channel_id=1, source_target_pairs={{0,2},{1,3},{2,0},{3,1},{4,6},{5,7},{6,4},{7,5},{8,10},{9,11},{10,... | collective-permute-start | bytes 602120 | tf_op jit(solution)/shard_map/ppermute | solution.py:34
  270.5 31.7 %collective-permute-start = (bf16[1,392,4,64]{1,3,2,0:T(8,128)(2,1)}, bf16[1,392,4,64]{1,3,2,0:T(8,128)(2,1)}, u32[]{:S(2)}, u32[]{:S(2)}) collective-permute-start(bf16[1,392,4,64]{1,3,2,0:T(8,128)(2,1)} %get-tuple-element.218), channel_id=1, source_target_pairs={{0,1},{1,2},{2,3},{3,0},{4,5},{5,6},{6,7},{7,4},{8,9},{9,10},{10,1... | collective-permute-start | bytes 602120 | tf_op jit(solution)/shard_map/ppermute | solution.py:34
  276.6 547.5 %reduce-scatter.7.cloned.1.call-start = ((), (), s32[]{:S(2)}) async-start(), calls=%async_computation.20 | async-start | bytes 4325376 | tf_op jit(solution)/shard_map/reduce_scatter | solution.py:294
  496.9 327.2 %reduce-scatter.9.cloned.1.call-start = ((), (), s32[]{:S(2)}) async-start(), calls=%async_computation.21 | async-start | bytes 4325376 | tf_op jit(solution)/shard_map/reduce_scatter | solution.py:296
  561.9 396.7 %reduce-scatter.11.cloned.1.call-start = ((), (), s32[]{:S(2)}) async-start(), calls=%async_computation.22 | async-start | bytes 4325376 | tf_op jit(solution)/shard_map/reduce_scatter | solution.py:297
  625.7 698.9 %reduce-scatter.15.cloned.1.call-start = ((), (), s32[]{:S(2)}) async-start(), calls=%async_computation.24 | async-start | bytes 17301504 | tf_op jit(solution)/shard_map/reduce_scatter | solution.py:303
  639.4 1050.1 %reduce-scatter.17.cloned.1.call-start = ((), (), s32[]{:S(2)}) async-start(), calls=%async_computation.25 | async-start | bytes 17301504 | tf_op jit(solution)/shard_map/reduce_scatter | solution.py:305
  694.2 37.9 %all-to-all-start.3 = ((bf16[4,2,50176]{2,1,0:T(2,128)(2,1)}), bf16[4,2,50176]{2,1,0:T(2,128)(2,1)S(1)}, u32[]{:S(2)}, u32[]{:S(2)}) async-start(bf16[4,2,50176]{2,1,0:T(2,128)(2,1)} %reshape.361), calls=%async_computation.3 | async-start | bytes 1605632 | tf_op jit(solution)/shard_map/all_to_all | solution.py:128
  (50 other events, 679.4 us)
Sparse Core Ops, SparseCore 0:
  9.9 30.5 all-gather.6
  42.4 27.8 all-gather.8
  72.2 27.8 all-gather.10
  101.9 27.8 all-gather.12
  131.6 54.4 all-gather.14
  187.8 54.3 all-gather.16
  276.7 152.5 reduce-scatter.12
  497.0 155.7 reduce-scatter.6
  655.6 153.8 reduce-scatter.8
  812.2 146.4 reduce-scatter.10
  961.5 363.0 reduce-scatter.14
  1327.3 362.1 reduce-scatter.16
